TPU v7x, 256 devices: a whole 4x4x8 slice. The times are simulated.
256 devices in a mesh: row: 4 (over y_lo, core), col: 64 (over x, y_hi, z).
Axes of the slice: x: 4, y: 4 (y_hi: 2, y_lo: 2; y = y_hi * 2 + y_lo), z: 8, core: 2. Of those that a mesh axis runs over, the one named last changes fastest.
Arguments:
- tensor: bfloat16 [128, 3072, 4096], P(None, 'col', 'row'), may hold values from -6 to 6
- first_factor: bfloat16 [64, 4096], P(None, ('row', 'col')), may hold values from -0.453125 to 0.453125
- second_factor: bfloat16 [64, 3072], P(None, 'col'), may hold values from -0.5232237 to 0.5232237
Outputs:
- frames: float32 [64, 128], replicated
- mode_one: float32 [64, 4096], P(None, ('row', 'col'))
All inputs are finite; a program needn't handle non-finite values.
Results may differ from a plain program's by a relative error of at most 0.004.
Values may be sent and summed in bfloat16 or wider, within the bound.
A program may use at most 128 MiB of HBM per device.

v0:
```python
import jax
import jax.numpy as jnp
from jax import lax
from jax.sharding import PartitionSpec as P

ridge_weight = 0.05


def ridge_solve(gram, right_side):
    order_size = gram.shape[0]
    factor_low = jnp.linalg.cholesky(gram + ridge_weight * jnp.eye(order_size, dtype=jnp.float32))
    middle = lax.linalg.triangular_solve(factor_low, right_side, left_side=True, lower=True)
    return lax.linalg.triangular_solve(
        factor_low, middle, left_side=True, lower=True, transpose_a=True
    )


def gram_of(factor):
    return jnp.dot(factor, factor.T, preferred_element_type=jnp.float32)


def spread_product(frames, second):
    product = frames[:, :, None] * second[:, None, :]
    return product.astype(jnp.bfloat16).reshape(frames.shape[0], -1)


def project_columns(flattened, portion):
    return lax.dot_general(
        portion, flattened, (((1,), (1,)), ((), ())), preferred_element_type=jnp.float32
    )


def local(tensor, first_factor, second_factor):
    frame_count, col_count, row_count = tensor.shape
    components = first_factor.shape[0]
    flattened = tensor.reshape(frame_count * col_count, row_count)
    second_values = second_factor.astype(jnp.float32)
    share_rows = row_count // lax.axis_size("col")
    gram_first = lax.psum(gram_of(first_factor), ("row", "col"))
    gram_second = lax.psum(gram_of(second_factor), "col")
    projected = project_columns(flattened, lax.all_gather(first_factor, "col", axis=1, tiled=True))
    projected = projected.reshape(components, frame_count, col_count)
    frame_part = jnp.einsum("rkj,rj->rk", projected, second_values, precision=lax.Precision.HIGHEST)
    frame_sum = lax.psum(frame_part, ("row", "col"))
    frames = ridge_solve(gram_first * gram_second, frame_sum)
    gram_frames = jnp.dot(frames, frames.T, precision=lax.Precision.HIGHEST)
    weights = spread_product(frames, second_values)
    full_part = lax.dot_general(
        weights, flattened, (((1,), (0,)), ((), ())), preferred_element_type=jnp.float32
    )
    first_sum = lax.psum(full_part, "col")
    new_first = ridge_solve(gram_second * gram_frames, first_sum).astype(jnp.bfloat16)
    gram_new = lax.psum(gram_of(new_first), "row")
    projected_new = lax.dot_general(
        new_first, flattened, (((1,), (1,)), ((), ())), preferred_element_type=jnp.float32
    )
    projected_new = projected_new.reshape(components, frame_count, col_count)
    second_part = jnp.einsum("rkj,rk->rj", projected_new, frames, precision=lax.Precision.HIGHEST)
    second_sum = lax.psum(second_part, "row")
    new_second = ridge_solve(gram_new * gram_frames, second_sum)
    weights_next = spread_product(frames, new_second)
    full_next = lax.dot_general(
        weights_next, flattened, (((1,), (0,)), ((), ())), preferred_element_type=jnp.float32
    )
    summed = lax.psum(full_next, "col")
    mode_one = lax.dynamic_slice_in_dim(summed, lax.axis_index("col") * share_rows, share_rows, 1)
    return (frames, mode_one)


def solution(mesh):
    return jax.shard_map(
        local,
        mesh=mesh,
        in_specs=(P(None, "col", "row"), P(None, ("row", "col")), P(None, "col")),
        out_specs=(P(), P(None, ("row", "col"))),
        check_vma=False,
    )
```

profile of v0, /device:TPU:8, one launch (start us, length us, event | category | flops | bytes accessed | tf_op | source)
XLA Modules:
  0.0 2033.9 jit_solution(1604844099440439791)
XLA Ops:
  7.2 0.0 all-reduce.5.cloned.1.call-start
  7.2 185.3 %all_gather.3 = bf16[64,1024]{0,1:T(8,128)(2,1)S(1)} all-gather(bf16[64,16]{0,1:T(8,128)(2,1)} %param.5), channel_id=1, replica_groups=mesh['row'=4,'col'=64] {'col'}, dimensions={1}, use_global_device_ids=true | all-gather | bytes 133120 | tf_op jit(solution)/shard_map/all_gather | solution.py:41
  192.5 0.9 fusion.29
  193.4 1.0 fusion.30
  194.4 0.7 convert_element_type.15
  195.1 0.0 copy-start.1
  195.1 17.8 copy.28
  212.9 0.0 copy-done.1
  212.9 0.1 copy.30
  213.0 350.9 %psum.50 = f32[64,64]{1,0:T(8,128)S(1)} all-reduce(f32[64,64]{1,0:T(8,128)S(1)} %fusion.30), channel_id=1, replica_groups=mesh['row'=4,'col'=64] {'col'}, use_global_device_ids=true, to_apply=%region_1.0 | all-reduce | flops 4096 | bytes 32768 | tf_op jit(solution)/shard_map/psum | solution.py:40
  563.9 6.9 fusion.8
  570.8 1.7 fusion.2
  572.5 72.5 %all-reduce = (f32[64,128]{1,0:T(8,128)S(1)}, f32[64,64]{1,0:T(8,128)S(1)}) all-reduce(f32[64,128]{1,0:T(8,128)S(1)} %bitcast.73, f32[64,64]{1,0:T(8,128)S(1)} %fusion.29), channel_id=1, replica_groups=mesh['row'=4,'col'=64] {'row','col'}, use_global_device_ids=true, to_apply=%region_4.0 | all-reduce | flops 12288 | bytes 98304 | tf_op jit(solution)/shard_map/psum | solution.py:44
  645.0 0.1 copy.19
  645.1 0.1 copy.20
  645.2 5.9 cholesky.59
  651.1 0.6 compare_reduce_fusion.2
  651.7 0.7 fusion.12
  652.4 4.9 custom-call.17
  657.3 0.3 fusion.26
  657.6 0.2 fusion.24
  657.7 0.0 copy-start
  657.7 7.6 convolution_bitcast_fusion.1
  665.3 0.0 all-reduce.5.cloned.1.call-update
  665.3 0.2 all-reduce.7.cloned.1.call-start
  665.5 0.2 select_add_fusion.1
  665.7 0.1 copy.22
  665.8 0.1 copy.23
  665.9 5.9 cholesky.70
  671.8 0.6 compare_reduce_fusion.1
  672.4 0.7 fusion.13
  673.1 4.9 custom-call.18
  678.0 619.7 %all-reduce.5.cloned.1.call-done = f32[64,1024]{1,0:T(8,128)} async-done(((f32[64,1024]{1,0:T(8,128)}), f32[64,1024]{1,0:T(8,128)}) %all-reduce.5.cloned.1.call-update) | async-done | bytes 262160 | tf_op jit(solution)/shard_map/psum | solution.py:51
  1297.7 1.4 fusion.21
  1299.1 0.4 convolution_convert_fusion
  1299.4 6.9 fusion.10
  1306.3 0.2 fusion.31
  1306.5 3.3 fusion
  1309.8 10.7 all-reduce.1
  1320.5 0.1 copy.25
  1320.6 0.1 copy.26
  1320.7 5.9 cholesky.81
  1326.6 0.6 compare_reduce_fusion
  1327.2 0.7 fusion.14
  1327.9 4.9 custom-call.19
  1332.8 0.2 fusion.17
  1333.0 0.2 fusion.15
  1333.2 0.0 copy-done
  1333.2 7.3 convolution_bitcast_fusion
  1340.6 0.0 all-reduce.7.cloned.1.call-update
  1340.6 685.2 %all-reduce.7.cloned.1.call-done = f32[64,1024]{0,1:T(8,128)} async-done(((f32[64,1024]{0,1:T(8,128)}), f32[64,1024]{0,1:T(8,128)}) %all-reduce.7.cloned.1.call-update) | async-done | bytes 262160 | tf_op jit(solution)/shard_map/psum | solution.py:65
  2025.8 1.3 constant_dynamic-slice_fusion
  (8 shorter events, 0.1 us)
Async XLA Ops:
  7.2 1290.5 %all-reduce.5.cloned.1.call-start = ((), (), s32[]{:S(2)}) async-start(), calls=%async_computation | async-start | bytes 524288 | tf_op jit(solution)/shard_map/psum | solution.py:51
  195.1 17.8 copy-start.1
  657.7 675.5 %copy-start = (f32[64,128]{1,0:T(8,128)}, f32[64,128]{1,0:T(8,128)S(1)}, u32[]{:S(2)}) copy-start(f32[64,128]{1,0:T(8,128)S(1)} %fusion.24) | copy-start | bytes 98308
  665.3 1360.5 %all-reduce.7.cloned.1.call-start = ((), (), s32[]{:S(2)}) async-start(), calls=%async_computation.1 | async-start | bytes 1048576 | tf_op jit(solution)/shard_map/psum | solution.py:65
Sparse Core Ops, SparseCore 0:
  665.4 632.2 all-reduce.4
  1340.7 685.0 all-reduce.6
where the time goes:
time: 2030 us
  waiting for transfers between devices  1300 us (64%)
  blocking collectives  619 us (30%)
  matrix products  38.5 us (2%)
  other arithmetic  37 us (2%)
    psum x1, waiting for transfers between devices, local(): summed = lax.psum(full_next, 'col')  685 us
    psum x1, waiting for transfers between devices, local(): first_sum = lax.psum(full_part, 'col')  620 us
    psum x1, blocking collectives, local(): gram_second = lax.psum(gram_of(second_factor), 'col')  351 us
    all_gather x1, blocking collectives, local(): lax.all_gather(first_factor, 'col', axis=1, tiled=True)  185 us
    psum x1, blocking collectives, local(): frame_sum = lax.psum(frame_part, ('row', 'col'))  72.5 us
  transfers between devices with their start and end apart: 2, of which 2 were waited for; matrix products, arithmetic and copies ran while one was open for 1% of the time, Pallas kernels for 0%

commit v1 on v0

--- a/solution.py
+++ b/solution.py
@@ -4,6 +4,15 @@
 from jax.sharding import PartitionSpec as P
 
 ridge_weight = 0.05
+
+
+def serve_the_teams(x_local, shard_axis):
+    sides = []
+    for _ in range(lax.axis_size(shard_axis)):
+        sides.append(x_local)
+    z2 = jnp.stack(sides)
+    w2 = lax.all_to_all(z2, shard_axis, 0, 0)
+    return jnp.concatenate(w2, axis=1)
 
 
 def ridge_solve(gram, right_side):
@@ -38,7 +47,7 @@
     share_rows = row_count // lax.axis_size("col")
     gram_first = lax.psum(gram_of(first_factor), ("row", "col"))
     gram_second = lax.psum(gram_of(second_factor), "col")
-    projected = project_columns(flattened, lax.all_gather(first_factor, "col", axis=1, tiled=True))
+    projected = project_columns(flattened, serve_the_teams(first_factor, "col"))
     projected = projected.reshape(components, frame_count, col_count)
     frame_part = jnp.einsum("rkj,rj->rk", projected, second_values, precision=lax.Precision.HIGHEST)
     frame_sum = lax.psum(frame_part, ("row", "col"))

time: 2030 us -> 1880 us (0.926)
  blocking collectives: 619 us -> 442 us
    all_gather x1 -> x0, blocking collectives: 185 us -> none  [local(): lax.all_gather(first_factor, 'col', axis=1, tiled=True)]
  transfers between devices with their start and end apart: 2 -> 3, of which waited for: 2 -> 2; matrix products, arithmetic and copies ran while one was open for 1% -> 1% of each run, Pallas kernels for 0% -> 0%
where the time goes in v1:
time: 1880 us
  waiting for transfers between devices  1310 us (70%)
  blocking collectives  442 us (24%)
  matrix products  37.7 us (2%)
  other arithmetic  37 us (2%)
  local copies, waits for them, and re-layouts  21.5 us (1%)
    psum x1, waiting for transfers between devices, local(): summed = lax.psum(full_next, 'col')  685 us
    psum x1, waiting for transfers between devices, local(): first_sum = lax.psum(full_part, 'col')  626 us
    psum x1, blocking collectives, local(): gram_second = lax.psum(gram_of(second_factor), 'col')  358 us
    psum x1, blocking collectives, local(): frame_sum = lax.psum(frame_part, ('row', 'col'))  72.5 us
  transfers between devices with their start and end apart: 3, of which 2 were waited for; matrix products, arithmetic and copies ran while one was open for 1% of the time, Pallas kernels for 0%

profile of v1, /device:TPU:8, one launch (start us, length us, event | category | flops | bytes accessed | tf_op | source)
XLA Modules:
  0.0 1876.9 jit_solution(18435310721203412004)
XLA Ops:
  7.2 0.0 copy-start
  7.2 0.7 copy-done
  7.9 0.9 reshape.54
  8.7 13.7 all-to-all-start
  22.4 0.0 all-reduce.5.cloned.1.call-start
  22.5 1.0 fusion.28
  23.4 0.7 convert_element_type.15
  24.1 0.0 copy-start.2
  24.1 17.8 copy.30
  42.0 0.0 copy-done.2
  42.0 0.1 copy.33
  42.1 358.4 %psum.50 = f32[64,64]{1,0:T(8,128)S(1)} all-reduce(f32[64,64]{1,0:T(8,128)S(1)} %fusion.28), channel_id=1, replica_groups=mesh['row'=4,'col'=64] {'col'}, use_global_device_ids=true, to_apply=%region_1.0 | all-reduce | flops 4096 | bytes 32768 | tf_op jit(solution)/shard_map/psum | solution.py:49
  400.5 0.2 fusion.27
  400.7 0.0 all-to-all-done
  400.7 0.2 reshape.55
  400.9 6.9 fusion.29
  407.8 1.7 fusion.2
  409.6 72.5 %all-reduce = (f32[64,128]{1,0:T(8,128)S(1)}, f32[64,64]{1,0:T(8,128)S(1)}) all-reduce(f32[64,128]{1,0:T(8,128)S(1)} %bitcast.80, f32[64,64]{1,0:T(8,128)S(1)} %fusion.27), channel_id=1, replica_groups=mesh['row'=4,'col'=64] {'row','col'}, use_global_device_ids=true, to_apply=%region_4.0 | all-reduce | flops 12288 | bytes 98304 | tf_op jit(solution)/shard_map/psum | solution.py:53
  482.0 0.1 copy.20
  482.1 0.1 copy.21
  482.2 5.9 cholesky.59
  488.1 0.6 compare_reduce_fusion.2
  488.8 0.7 fusion.10
  489.4 4.9 custom-call.17
  494.3 0.3 fusion.24
  494.6 0.2 fusion.22
  494.7 0.0 copy-start.1
  494.7 0.2 select_add_fusion.1
  494.9 0.1 copy.24
  495.0 0.1 copy.25
  495.1 5.9 cholesky.70
  501.0 7.6 convolution_bitcast_fusion.1
  508.6 0.0 all-reduce.5.cloned.1.call-update
  508.6 0.2 all-reduce.7.cloned.1.call-start
  508.8 0.6 compare_reduce_fusion.1
  509.5 0.7 fusion.11
  510.1 4.9 custom-call.18
  515.0 625.9 %all-reduce.5.cloned.1.call-done = f32[64,1024]{1,0:T(8,128)} async-done(((f32[64,1024]{1,0:T(8,128)}), f32[64,1024]{1,0:T(8,128)}) %all-reduce.5.cloned.1.call-update) | async-done | bytes 262160 | tf_op jit(solution)/shard_map/psum | solution.py:60
  1140.9 1.4 fusion.19
  1142.3 0.4 convolution_convert_fusion
  1142.6 6.9 fusion.8
  1149.5 0.2 fusion.30
  1149.7 3.3 fusion
  1153.0 10.7 all-reduce.1
  1163.7 0.1 copy.27
  1163.8 0.1 copy.28
  1163.9 5.9 cholesky.81
  1169.8 0.6 compare_reduce_fusion
  1170.4 0.7 fusion.12
  1171.1 4.9 custom-call.19
  1176.0 0.2 fusion.15
  1176.3 0.2 fusion.13
  1176.4 0.0 copy-done.1
  1176.5 7.3 convolution_bitcast_fusion
  1183.8 0.0 all-reduce.7.cloned.1.call-update
  1183.8 684.9 %all-reduce.7.cloned.1.call-done = f32[64,1024]{0,1:T(8,128)} async-done(((f32[64,1024]{0,1:T(8,128)}), f32[64,1024]{0,1:T(8,128)}) %all-reduce.7.cloned.1.call-update) | async-done | bytes 262160 | tf_op jit(solution)/shard_map/psum | solution.py:74
  1868.7 1.3 constant_dynamic-slice_fusion
  (9 shorter events, 0.2 us)
Async XLA Ops:
  7.2 0.7 copy-start
  8.7 392.0 %all-to-all-start = ((bf16[64,2,512]{2,1,0:T(2,128)(2,1)}), bf16[64,2,512]{2,1,0:T(2,128)(2,1)S(1)}, u32[]{:S(2)}, u32[]{:S(2)}) async-start(bf16[64,2,512]{2,1,0:T(2,128)(2,1)} %reshape.54), calls=%async_computation | async-start | bytes 262144 | tf_op jit(solution)/shard_map/all_to_all | solution.py:14
  22.4 1118.5 %all-reduce.5.cloned.1.call-start = ((), (), s32[]{:S(2)}) async-start(), calls=%async_computation.1 | async-start | bytes 524288 | tf_op jit(solution)/shard_map/psum | solution.py:60
  24.1 17.8 copy-start.2
  494.7 681.7 %copy-start.1 = (f32[64,128]{1,0:T(8,128)}, f32[64,128]{1,0:T(8,128)S(1)}, u32[]{:S(2)}) copy-start(f32[64,128]{1,0:T(8,128)S(1)} %fusion.22) | copy-start | bytes 98308
  508.6 1360.2 %all-reduce.7.cloned.1.call-start = ((), (), s32[]{:S(2)}) async-start(), calls=%async_computation.2 | async-start | bytes 1048576 | tf_op jit(solution)/shard_map/psum | solution.py:74
Sparse Core Ops, SparseCore 0:
  508.7 632.1 all-reduce.4
  1183.9 684.7 all-reduce.6

commit v2 on v0

--- a/solution.py
+++ b/solution.py
@@ -41,7 +41,7 @@
     projected = project_columns(flattened, lax.all_gather(first_factor, "col", axis=1, tiled=True))
     projected = projected.reshape(components, frame_count, col_count)
     frame_part = jnp.einsum("rkj,rj->rk", projected, second_values, precision=lax.Precision.HIGHEST)
-    frame_sum = lax.psum(frame_part, ("row", "col"))
+    frame_sum = lax.psum(lax.psum(frame_part, axis_name="row"), axis_name="col")
     frames = ridge_solve(gram_first * gram_second, frame_sum)
     gram_frames = jnp.dot(frames, frames.T, precision=lax.Precision.HIGHEST)
     weights = spread_product(frames, second_values)

time: 2030 us -> 2040 us (level)
    psum x2 -> x3, blocking collectives: 423 us -> 437 us  [the longest x2 364 us: local(): frame_sum = lax.psum(lax.psum(frame_part, axis_name='row'), axis_name='col')]
where the time goes in v2:
time: 2040 us
  waiting for transfers between devices  1300 us (64%)
  blocking collectives  633 us (31%)
  matrix products  38.5 us (2%)
  other arithmetic  37 us (2%)
    psum x1, waiting for transfers between devices, local(): summed = lax.psum(full_next, 'col')  685 us
    psum x1, waiting for transfers between devices, local(): first_sum = lax.psum(full_part, 'col')  616 us
    psum x2, blocking collectives, local(): frame_sum = lax.psum(lax.psum(frame_part, axis_name='row'), axis_name='col')  364 us
    all_gather x1, blocking collectives, local(): lax.all_gather(first_factor, 'col', axis=1, tiled=True)  185 us
    psum x1, blocking collectives, local(): gram_first = lax.psum(gram_of(first_factor), ('row', 'col'))  72.5 us
  transfers between devices with their start and end apart: 2, of which 2 were waited for; matrix products, arithmetic and copies ran while one was open for 1% of the time, Pallas kernels for 0%

profile of v2, /device:TPU:8, one launch (start us, length us, event | category | flops | bytes accessed | tf_op | source)
XLA Modules:
  0.0 2043.6 jit_solution(8261557259844210761)
XLA Ops:
  7.2 0.0 all-reduce.5.cloned.1.call-start
  7.2 185.3 %all_gather.3 = bf16[64,1024]{0,1:T(8,128)(2,1)S(1)} all-gather(bf16[64,16]{0,1:T(8,128)(2,1)} %param.5), channel_id=1, replica_groups=mesh['row'=4,'col'=64] {'col'}, dimensions={1}, use_global_device_ids=true | all-gather | bytes 133120 | tf_op jit(solution)/shard_map/all_gather | solution.py:41
  192.5 0.9 fusion.29
  193.4 1.0 fusion.30
  194.4 0.7 convert_element_type.15
  195.1 0.0 copy-start.1
  195.1 17.8 copy.28
  212.9 0.0 copy-done.1
  212.9 0.1 copy.30
  213.0 6.9 fusion.8
  219.9 1.7 fusion.2
  221.7 10.3 psum.58
  231.9 72.5 %psum.56 = f32[64,64]{1,0:T(8,128)S(1)} all-reduce(f32[64,64]{1,0:T(8,128)S(1)} %fusion.29), channel_id=1, replica_groups=mesh['row'=4,'col'=64] {'row','col'}, use_global_device_ids=true, to_apply=%region_0.0 | all-reduce | flops 4096 | bytes 32768 | tf_op jit(solution)/shard_map/psum | solution.py:39
  304.4 353.9 %all-reduce = (f32[64,128]{1,0:T(8,128)S(1)}, f32[64,64]{1,0:T(8,128)S(1)}) all-reduce(f32[64,128]{1,0:T(8,128)S(1)} %psum.58, f32[64,64]{1,0:T(8,128)S(1)} %fusion.30), channel_id=1, replica_groups=mesh['row'=4,'col'=64] {'col'}, use_global_device_ids=true, to_apply=%region_5.0 | all-reduce | flops 12288 | bytes 98304 | tf_op jit(solution)/shard_map/psum | solution.py:44
  658.3 0.1 copy.19
  658.4 0.1 copy.20
  658.5 5.9 cholesky.59
  664.4 0.6 compare_reduce_fusion.2
  665.0 0.7 fusion.12
  665.7 4.9 custom-call.17
  670.6 0.3 fusion.26
  670.9 0.2 fusion.24
  671.0 0.0 copy-start
  671.0 7.6 convolution_bitcast_fusion.1
  678.6 0.0 all-reduce.5.cloned.1.call-update
  678.6 0.2 all-reduce.7.cloned.1.call-start
  678.9 0.2 select_add_fusion.1
  679.1 0.1 copy.22
  679.1 0.1 copy.23
  679.2 5.9 cholesky.70
  685.1 0.6 compare_reduce_fusion.1
  685.8 0.7 fusion.13
  686.4 4.9 custom-call.18
  691.3 616.3 %all-reduce.5.cloned.1.call-done = f32[64,1024]{1,0:T(8,128)} async-done(((f32[64,1024]{1,0:T(8,128)}), f32[64,1024]{1,0:T(8,128)}) %all-reduce.5.cloned.1.call-update) | async-done | bytes 262160 | tf_op jit(solution)/shard_map/psum | solution.py:51
  1307.6 1.4 fusion.21
  1308.9 0.4 convolution_convert_fusion
  1309.3 6.9 fusion.10
  1316.2 0.2 fusion.31
  1316.4 3.3 fusion
  1319.7 10.7 all-reduce.1
  1330.4 0.1 copy.25
  1330.5 0.1 copy.26
  1330.6 5.9 cholesky.81
  1336.5 0.6 compare_reduce_fusion
  1337.1 0.7 fusion.14
  1337.8 4.9 custom-call.19
  1342.7 0.2 fusion.17
  1342.9 0.2 fusion.15
  1343.1 0.0 copy-done
  1343.1 7.3 convolution_bitcast_fusion
  1350.5 0.0 all-reduce.7.cloned.1.call-update
  1350.5 684.9 %all-reduce.7.cloned.1.call-done = f32[64,1024]{0,1:T(8,128)} async-done(((f32[64,1024]{0,1:T(8,128)}), f32[64,1024]{0,1:T(8,128)}) %all-reduce.7.cloned.1.call-update) | async-done | bytes 262160 | tf_op jit(solution)/shard_map/psum | solution.py:65
  2035.4 1.3 constant_dynamic-slice_fusion
  (8 shorter events, 0.1 us)
Async XLA Ops:
  7.2 1300.4 %all-reduce.5.cloned.1.call-start = ((), (), s32[]{:S(2)}) async-start(), calls=%async_computation | async-start | bytes 524288 | tf_op jit(solution)/shard_map/psum | solution.py:51
  195.1 17.8 copy-start.1
  671.0 672.1 %copy-start = (f32[64,128]{1,0:T(8,128)}, f32[64,128]{1,0:T(8,128)S(1)}, u32[]{:S(2)}) copy-start(f32[64,128]{1,0:T(8,128)S(1)} %fusion.24) | copy-start | bytes 98308
  678.6 1356.8 %all-reduce.7.cloned.1.call-start = ((), (), s32[]{:S(2)}) async-start(), calls=%async_computation.1 | async-start | bytes 1048576 | tf_op jit(solution)/shard_map/psum | solution.py:65
Sparse Core Ops, SparseCore 0:
  678.8 628.7 all-reduce.4
  1350.6 684.7 all-reduce.6

commit v3 on v0

--- a/solution.py
+++ b/solution.py
@@ -4,6 +4,12 @@
 from jax.sharding import PartitionSpec as P
 
 ridge_weight = 0.05
+
+
+def gather_and_add(value, axis):
+    terms = lax.all_gather(value, axis, axis=0, tiled=False)
+    total = terms.sum(axis=0)
+    return total
 
 
 def ridge_solve(gram, right_side):
@@ -41,7 +47,7 @@
     projected = project_columns(flattened, lax.all_gather(first_factor, "col", axis=1, tiled=True))
     projected = projected.reshape(components, frame_count, col_count)
     frame_part = jnp.einsum("rkj,rj->rk", projected, second_values, precision=lax.Precision.HIGHEST)
-    frame_sum = lax.psum(frame_part, ("row", "col"))
+    frame_sum = gather_and_add(frame_part, ("row", "col"))
     frames = ridge_solve(gram_first * gram_second, frame_sum)
     gram_frames = jnp.dot(frames, frames.T, precision=lax.Precision.HIGHEST)
     weights = spread_product(frames, second_values)

time: 2030 us -> 2320 us (1.14)
  waiting for transfers between devices: 1300 us -> 1580 us
    all_gather x0 -> x1, waiting for transfers between devices: none -> 245 us  [gather_and_add(): terms = lax.all_gather(value, axis, axis=0, tiled=False)]
    psum x1, waiting for transfers between devices: 620 us -> 651 us  [local(): first_sum = lax.psum(full_part, 'col')]
  transfers between devices with their start and end apart: 2 -> 3, of which waited for: 2 -> 3; matrix products, arithmetic and copies ran while one was open for 1% -> 1% of each run, Pallas kernels for 0% -> 0%
where the time goes in v3:
time: 2320 us
  waiting for transfers between devices  1580 us (68%)
  blocking collectives  621 us (27%)
  other arithmetic  40.2 us (2%)
  matrix products  37.6 us (2%)
    psum x1, waiting for transfers between devices, local(): summed = lax.psum(full_next, 'col')  685 us
    psum x1, waiting for transfers between devices, local(): first_sum = lax.psum(full_part, 'col')  651 us
    psum x1, blocking collectives, local(): gram_second = lax.psum(gram_of(second_factor), 'col')  354 us
    all_gather x1, waiting for transfers between devices, gather_and_add(): terms = lax.all_gather(value, axis, axis=0, tiled=False)  245 us
    all_gather x1, blocking collectives, local(): lax.all_gather(first_factor, 'col', axis=1, tiled=True)  185 us
    psum x1, blocking collectives, local(): gram_first = lax.psum(gram_of(first_factor), ('row', 'col'))  72.1 us
  transfers between devices with their start and end apart: 3, of which 3 were waited for; matrix products, arithmetic and copies ran while one was open for 1% of the time, Pallas kernels for 0%

profile of v3, /device:TPU:8, one launch (start us, length us, event | category | flops | bytes accessed | tf_op | source)
XLA Modules:
  0.0 2315.6 jit_solution(5932671018374344517)
XLA Ops:
  7.2 0.0 all-gather.3.cloned.1.call-start
  7.2 0.8 copy.30
  8.0 0.0 copy-start.2
  8.0 17.8 copy.28
  25.9 0.0 copy-done.2
  25.9 185.0 %all_gather.9 = bf16[64,1024]{0,1:T(8,128)(2,1)S(1)} all-gather(bf16[64,16]{0,1:T(8,128)(2,1)S(1)} %copy-done.2), channel_id=1, replica_groups=mesh['row'=4,'col'=64] {'col'}, dimensions={1}, use_global_device_ids=true | all-gather | bytes 133120 | tf_op jit(solution)/shard_map/all_gather | solution.py:47
  210.9 6.9 fusion.8
  217.8 0.0 copy-start.1
  217.8 2.3 fusion.2
  220.1 0.0 all-gather.3.cloned.1.call-update
  220.2 0.0 all-reduce.4.cloned.1.call-start
  220.2 0.0 copy-done.1
  220.2 0.2 fusion.29
  220.4 72.1 %psum.42 = f32[64,64]{1,0:T(8,128)S(1)} all-reduce(f32[64,64]{1,0:T(8,128)S(1)} %fusion.29), channel_id=1, replica_groups=mesh['row'=4,'col'=64] {'row','col'}, use_global_device_ids=true, to_apply=%region_0.0 | all-reduce | flops 4096 | bytes 32768 | tf_op jit(solution)/shard_map/psum | solution.py:45
  292.5 0.2 fusion.30
  292.7 353.5 %psum.43 = f32[64,64]{1,0:T(8,128)S(1)} all-reduce(f32[64,64]{1,0:T(8,128)S(1)} %fusion.30), channel_id=1, replica_groups=mesh['row'=4,'col'=64] {'col'}, use_global_device_ids=true, to_apply=%region_1.0 | all-reduce | flops 4096 | bytes 32768 | tf_op jit(solution)/shard_map/psum | solution.py:46
  646.3 0.1 copy.19
  646.4 0.1 copy.20
  646.4 5.9 cholesky.59
  652.3 0.6 compare_reduce_fusion.2
  653.0 0.7 fusion.12
  653.6 4.9 custom-call.17
  658.5 245.2 %all-gather.3.cloned.1.call-done = f32[16384,128]{1,0:T(8,128)} async-done(((f32[64,128]{1,0:T(8,128)}), f32[16384,128]{1,0:T(8,128)}) %all-gather.3.cloned.1.call-update) | async-done | bytes 8388624 | tf_op jit(solution)/shard_map/all_gather | solution.py:10
  903.7 3.9 reduce_sum.9
  907.7 0.2 fusion.26
  907.9 0.2 fusion.24
  908.1 0.0 copy-start
  908.1 0.2 select_add_fusion.1
  908.3 7.6 convolution_bitcast_fusion.1
  915.8 0.0 all-reduce.4.cloned.1.call-update
  915.8 0.2 all-reduce.6.cloned.1.call-start
  916.1 0.1 copy.22
  916.2 0.1 copy.23
  916.2 5.9 cholesky.70
  922.1 0.6 compare_reduce_fusion.1
  922.8 0.7 fusion.13
  923.4 4.9 custom-call.18
  928.3 651.3 %all-reduce.4.cloned.1.call-done = f32[64,1024]{1,0:T(8,128)} async-done(((f32[64,1024]{1,0:T(8,128)}), f32[64,1024]{1,0:T(8,128)}) %all-reduce.4.cloned.1.call-update) | async-done | bytes 262160 | tf_op jit(solution)/shard_map/psum | solution.py:57
  1579.7 1.4 fusion.21
  1581.0 0.4 convolution_convert_fusion
  1581.4 6.9 fusion.10
  1588.3 0.2 fusion.31
  1588.4 3.3 fusion
  1591.8 10.7 all-reduce
  1602.5 0.1 copy.25
  1602.6 0.1 copy.26
  1602.7 5.9 cholesky.81
  1608.6 0.6 compare_reduce_fusion
  1609.2 0.7 fusion.14
  1609.9 4.9 custom-call.19
  1614.8 0.2 fusion.17
  1615.0 0.2 fusion.15
  1615.2 0.0 copy-done
  1615.2 7.3 convolution_bitcast_fusion
  1622.6 0.0 all-reduce.6.cloned.1.call-update
  1622.6 685.2 %all-reduce.6.cloned.1.call-done = f32[64,1024]{0,1:T(8,128)} async-done(((f32[64,1024]{0,1:T(8,128)}), f32[64,1024]{0,1:T(8,128)}) %all-reduce.6.cloned.1.call-update) | async-done | bytes 262160 | tf_op jit(solution)/shard_map/psum | solution.py:71
  2307.8 1.3 constant_dynamic-slice_fusion
  (9 shorter events, 0.1 us)
Async XLA Ops:
  7.2 896.6 %all-gather.3.cloned.1.call-start = ((), (), s32[]{:S(2)}) async-start(), calls=%async_computation.2 | async-start | bytes 8421376 | tf_op jit(solution)/shard_map/all_gather | solution.py:10
  8.0 17.8 copy-start.2
  217.8 2.4 copy-start.1
  220.2 1359.5 %all-reduce.4.cloned.1.call-start = ((), (), s32[]{:S(2)}) async-start(), calls=%async_computation | async-start | bytes 524288 | tf_op jit(solution)/shard_map/psum | solution.py:57
  908.1 707.1 %copy-start = (f32[64,128]{1,0:T(8,128)}, f32[64,128]{1,0:T(8,128)S(1)}, u32[]{:S(2)}) copy-start(f32[64,128]{1,0:T(8,128)S(1)} %fusion.24) | copy-start | bytes 98308
  915.8 1391.9 %all-reduce.6.cloned.1.call-start = ((), (), s32[]{:S(2)}) async-start(), calls=%async_computation.1 | async-start | bytes 1048576 | tf_op jit(solution)/shard_map/psum | solution.py:71
Sparse Core Ops, SparseCore 0:
  220.3 683.4 all-gather.2
  916.0 663.6 all-reduce.3
  1622.7 685.0 all-reduce.5
